TPU v7x, 128 devices: a whole 4x4x4 slice. The times are simulated.
128 devices in a mesh: seq: 32 (over x, y, core), head: 4 (over z).
Axes of the slice: x: 4, y: 4, z: 4, core: 2. Of those that a mesh axis runs over, the one named last changes fastest.
Arguments:
- queries: bfloat16 [65536, 4096], P('seq', 'head'), may hold values from -2 to 2
- key_rows: bfloat16 [65536, 4096], P('seq', 'head'), may hold values from -2 to 2
- value_rows: bfloat16 [65536, 4096], P('seq', 'head'), may hold values from -128 to 128
- decay_log: float32 [32, 65536], P('head', 'seq'), may hold values from -0.8 to 0
- norm_gain: float32 [4096], P('head'), may hold values from 0.1 to 1.9
- page_owner: int32 [64], replicated, may hold values from 0 to 31, as said below
Outputs:
- attended: bfloat16 [65536, 4096], P('seq', 'head')
- page_cache: bfloat16 [160, 32, 128, 128], P('seq', 'head')
Inputs may be any that keep to these rules, and one draw needn't show every extreme that they name: `page_owner`: the 2 pages p = i * 2 to (i + 1) * 2 - 1 have different owners for every i; no owner keeps more than 5 pages and one keeps exactly 5.
All inputs are finite; a program needn't handle non-finite values.
Results may differ from a plain program's by a relative error of at most 0.0042.
Values may be sent and summed in bfloat16 or wider, within the bound.
A program may use at most 128 MiB of HBM per device.

v0:
```python
import jax
import jax.numpy as jnp
from jax import lax
from jax.sharding import PartitionSpec as P

BLOCK = 512
PAGE = 1024
SLOTS = 5


def from_behind(value, axis, steps):
    count = lax.axis_size(axis)
    first, last = (max(0, -steps), min(count, count - steps))
    return lax.ppermute(value, axis, [(source, source + steps) for source in range(first, last)])


def block_terms(query_blk, key_blk, value_blk, cumulative, carry_state):
    length = cumulative.shape[1]
    token_positions = jnp.arange(length)
    causal = (token_positions[:, None] >= token_positions[None, :])[None]
    spread = cumulative[:, :, None] - cumulative[:, None, :]
    damping = jnp.where(causal, jnp.exp(jnp.where(causal, spread, 0.0)), 0.0)
    scores = jnp.einsum("thd,shd->hts", query_blk, key_blk, preferred_element_type=jnp.float32)
    weights = (scores * damping).astype(jnp.bfloat16)
    inner_sum = jnp.einsum("hts,shd->thd", weights, value_blk, preferred_element_type=jnp.float32)
    carried = jnp.einsum(
        "thd,hde->the", query_blk.astype(jnp.float32), carry_state, precision=lax.Precision.HIGHEST
    )
    output = inner_sum + carried * jnp.exp(cumulative).T[:, :, None]
    scaled_keys = (
        key_blk.astype(jnp.float32) * jnp.exp(cumulative[:, -1:] - cumulative).T[:, :, None]
    ).astype(jnp.bfloat16)
    update = jnp.einsum("shd,she->hde", scaled_keys, value_blk, preferred_element_type=jnp.float32)
    new_state = jnp.exp(cumulative[:, -1])[:, None, None] * carry_state + update
    return (output, new_state)


def combine(earlier, following):
    return (
        earlier[0] + following[0],
        jnp.exp(following[0])[:, None, None] * earlier[1] + following[1],
    )


def shards(queries, key_rows, value_rows, decay_log, norm_gain, page_owner):
    tok_rows, width_dev = queries.shape
    head_count = decay_log.shape[0]
    head_dim = width_dev // head_count
    block_count = tok_rows // BLOCK
    grid_shape = (block_count, BLOCK, head_count, head_dim)
    query_blocks = queries.reshape(grid_shape)
    key_blocks = key_rows.reshape(grid_shape)
    value_blocks = value_rows.reshape(grid_shape)
    cumulative = jnp.cumsum(decay_log.reshape(head_count, block_count, BLOCK), axis=2)
    block_decay = cumulative[:, :, -1]
    reached = jnp.cumsum(block_decay, axis=1)

    def local_step(carry_state, pieces):
        query_blk, key_blk, value_blk, decay_blk = pieces
        output, new_state = block_terms(query_blk, key_blk, value_blk, decay_blk, carry_state)
        return (new_state, (output, new_state))

    zero_state = jnp.zeros((head_count, head_dim, head_dim), jnp.float32)
    local_end, (local_out, block_states) = lax.scan(
        local_step,
        zero_state,
        (query_blocks, key_blocks, value_blocks, cumulative.transpose(1, 0, 2)),
    )
    own_part = (reached[:, -1], local_end)
    identity = (jnp.zeros((head_count,), jnp.float32), zero_state)

    def relay_turn(turn_index, incoming):
        return from_behind(combine(incoming, own_part), "seq", 1)

    incoming = lax.fori_loop(0, lax.axis_size("seq") - 1, relay_turn, identity)
    entry_state = incoming[1]
    start_log = reached - block_decay
    total_log = (cumulative + start_log[:, :, None]).reshape(head_count, tok_rows).T
    entry_term = jnp.einsum(
        "thd,hde->the",
        queries.reshape(tok_rows, head_count, head_dim).astype(jnp.float32),
        entry_state,
        precision=lax.Precision.HIGHEST,
    )
    output = (
        local_out.reshape(tok_rows, head_count, head_dim)
        + entry_term * jnp.exp(total_log)[:, :, None]
    )
    square_sum = jnp.sum(output * output, axis=(1, 2))
    total_square = lax.psum(square_sum, "head")
    scale_row = lax.rsqrt(total_square / (head_count * head_dim * lax.axis_size("head")) + 1e-06)
    normed = output * scale_row[:, None, None] * norm_gain.reshape(head_count, head_dim)[None]
    attended = normed.astype(jnp.bfloat16).reshape(tok_rows, width_dev)
    per_page = PAGE // BLOCK
    page_decay = jnp.exp(reached[:, per_page - 1 :: per_page]).T
    snapshots = (
        page_decay[:, :, None, None] * entry_state[None] + block_states[per_page - 1 :: per_page]
    ).astype(jnp.bfloat16)
    page_order = jnp.arange(page_owner.shape[0])
    earlier = (page_owner[:, None] == page_owner[None, :]) & (
        page_order[None, :] < page_order[:, None]
    )
    slot_index = jnp.sum(earlier.astype(jnp.int32), axis=1)
    seq_index = lax.axis_index("seq")
    slot_ids = jnp.arange(SLOTS)
    chosen = (page_owner[None, :] == seq_index) & (slot_index[None, :] == slot_ids[:, None])
    gathered = jnp.einsum(
        "sn,nhde->shde",
        chosen.astype(jnp.bfloat16),
        lax.all_gather(snapshots, "seq", axis=0, tiled=True),
        preferred_element_type=jnp.float32,
    )
    page_cache = gathered.astype(jnp.bfloat16)
    return (attended, page_cache)


def solution(mesh):
    return jax.shard_map(
        shards,
        mesh=mesh,
        in_specs=(
            P("seq", "head"),
            P("seq", "head"),
            P("seq", "head"),
            P("head", "seq"),
            P("head"),
            P(),
        ),
        out_specs=(P("seq", "head"), P("seq", "head", None, None)),
        check_vma=False,
    )
```

profile of v0, /device:TPU:1, one launch (start us, length us, event | category | flops | bytes accessed | tf_op | source)
XLA Modules:
  0.0 800.7 jit_solution(18202910825025236144)
XLA Ops:
  27.2 248.2 %while.28 = (s32[]{:T(128)}, f32[8,128,128]{2,1,0:T(8,128)}, f32[4,512,8,128]{1,0,3,2:T(4,128)}, f32[4,8,128,128]{3,2,1,0:T(8,128)}, f32[4,8,512]{2,1,0:T(8,128)...) while((s32[]{:T(128)}, f32[8,128,128]{2,1,0:T(8,128)}, ...), condition=%wide.region_3.4_spmd.clone, body=%wide.region_2.3_spmd.clone.sunk | while | flops 2027163648 | bytes 38535560 | solution.py:64
  48.1 41.0 %dynamic_update_slice.14 = f32[4,512,8,128]{1,0,3,2:T(4,128)} dynamic-update-slice(f32[4,512,8,128]{1,0,3,2:T(4,128)} %get-tuple-element.309, f32[1,512,8,128]{1,0,3,2:T(1,128)} %copy.188, s32[]{:T(128)S(6)} %copy.195, s32[]{:T(128)} %constant.44.clone.1..sunk, s32[]{:T(128)} %constant.44.clone.1..sunk, s32[]{:T(128)} %constant.44.clone.1..sunk) | dynamic-update-slice | bytes 4194308 | tf_op jit(solution)/shard_map/while/body/jit(dynamic_update_index_in_dim)/dynamic_update_slice | solution.py:64
  110.2 41.0 %dynamic_update_slice.14 = f32[4,512,8,128]{1,0,3,2:T(4,128)} dynamic-update-slice(f32[4,512,8,128]{1,0,3,2:T(4,128)} %get-tuple-element.309, f32[1,512,8,128]{1,0,3,2:T(1,128)} %copy.188, s32[]{:T(128)S(6)} %copy.195, s32[]{:T(128)} %constant.44.clone.1..sunk, s32[]{:T(128)} %constant.44.clone.1..sunk, s32[]{:T(128)} %constant.44.clone.1..sunk) | dynamic-update-slice | bytes 4194308 | tf_op jit(solution)/shard_map/while/body/jit(dynamic_update_index_in_dim)/dynamic_update_slice | solution.py:64
  172.3 41.0 %dynamic_update_slice.14 = f32[4,512,8,128]{1,0,3,2:T(4,128)} dynamic-update-slice(f32[4,512,8,128]{1,0,3,2:T(4,128)} %get-tuple-element.309, f32[1,512,8,128]{1,0,3,2:T(1,128)} %copy.188, s32[]{:T(128)S(6)} %copy.195, s32[]{:T(128)} %constant.44.clone.1..sunk, s32[]{:T(128)} %constant.44.clone.1..sunk, s32[]{:T(128)} %constant.44.clone.1..sunk) | dynamic-update-slice | bytes 4194308 | tf_op jit(solution)/shard_map/while/body/jit(dynamic_update_index_in_dim)/dynamic_update_slice | solution.py:64
  234.4 41.0 %dynamic_update_slice.14 = f32[4,512,8,128]{1,0,3,2:T(4,128)} dynamic-update-slice(f32[4,512,8,128]{1,0,3,2:T(4,128)} %get-tuple-element.309, f32[1,512,8,128]{1,0,3,2:T(1,128)} %copy.188, s32[]{:T(128)S(6)} %copy.195, s32[]{:T(128)} %constant.44.clone.1..sunk, s32[]{:T(128)} %constant.44.clone.1..sunk, s32[]{:T(128)} %constant.44.clone.1..sunk) | dynamic-update-slice | bytes 4194308 | tf_op jit(solution)/shard_map/while/body/jit(dynamic_update_index_in_dim)/dynamic_update_slice | solution.py:64
  276.1 388.3 %while.27 = (s32[]{:T(128)}, f32[8,128,128]{2,1,0:T(8,128)S(1)}, f32[8,1,1]{0,2,1:T(1,128)}, f32[8,128,128]{2,1,0:T(8,128)}, s32[]{:T(128)}) while((s32[]{:T(128)}, f32[8,128,128]{2,1,0:T(8,128)S(1)}, f32[8,1,1]{0,2,1:T(1,128)}, f32[8,128,128]{2,1,0:T(8,128)}, s32[]{:T(128)}) %tuple.70), condition=%wide.region_6.7_spmd, body=%wide.region_5.6_spmd.sunk | while | flops 262146 | bytes 3670149 | solution.py:75
  282.0 6.1 collective-permute-done
  293.7 6.1 collective-permute-done
  305.3 6.1 collective-permute-done
  317.0 6.1 collective-permute-done
  328.7 6.1 collective-permute-done
  340.3 6.1 collective-permute-done
  352.0 6.1 collective-permute-done
  363.7 6.1 collective-permute-done
  500.3 6.5 collective-permute-start
  514.0 6.5 collective-permute-start
  527.8 6.5 collective-permute-start
  541.6 6.5 collective-permute-start
  555.4 6.5 collective-permute-start
  569.1 6.5 collective-permute-start
  582.9 6.5 collective-permute-start
  596.7 6.5 collective-permute-start
  610.4 6.5 collective-permute-start
  624.2 6.5 collective-permute-start
  638.0 6.5 collective-permute-start
  651.8 6.5 collective-permute-start
  665.4 10.9 %reshape.92 = f32[2048,8,128]{0,2,1:T(8,128)} reshape(f32[4,512,8,128]{1,0,3,2:T(4,128)} %get-tuple-element.96) | data formatting | bytes 16777216 | tf_op jit(solution)/shard_map/reshape | solution.py:86
  677.5 12.3 %multiply_reduce_fusion = (f32[2048]{0:T(1024)S(1)}, f32[2048,8,128]{0,2,1:T(8,128)}) fusion(f32[2048,8,128]{0,2,1:T(8,128)} %reshape.92, f32[2048,8]{0,1:T(8,128)S(1)} %exponential_bitcast_fusion.2, f32[8,128,128]{2,1,0:T(8,128)S(1)} %get-tuple-element.98, bf16[2048,1024]{1,0:T(8,128)(2,1)} %param.10), kind=kOutput, calls=%fused_computation.34 | convolution fusion | flops 3229612032 | bytes 21569536 | tf_op jit(solution)/shard_map/thd,hde->the/dot_general | solution.py:79
  689.8 9.8 %psum.7 = f32[2048]{0:T(1024)S(1)} all-reduce(f32[2048]{0:T(1024)S(1)} %get-tuple-element.209), channel_id=1, replica_groups=mesh['seq'=32,'head'=4] {'head'}, use_global_device_ids=true, to_apply=%region_8.9 | all-reduce | flops 2048 | bytes 16384 | tf_op jit(solution)/shard_map/psum | solution.py:90
  705.7 6.4 copy.116
  712.3 65.4 %all-gather.2.cloned.1.call-done = bf16[64,8,128,128]{3,2,1,0:T(8,128)(2,1)} async-done(((bf16[2,8,128,128]{3,2,1,0:T(8,128)(2,1)}), bf16[64,8,128,128]{3,2,1,0:T(8,128)(2,1)}) %all-gather.2.cloned.1.call-update) | async-done | bytes 16777232 | tf_op jit(solution)/shard_map/all_gather | solution.py:110
  777.7 14.7 %fusion.18 = bf16[5,8,128,128]{3,0,2,1:T(8,128)(2,1)S(1)} fusion(bf16[64,8,128,128]{3,2,1,0:T(8,128)(2,1)} %all-gather.2.cloned.1.call-done, s32[64]{0:T(128)S(1)} %convert_reduce_fusion, pred[64]{0:T(512)(128)(4,1)S(1)} %broadcast_compare_fusion), kind=kOutput, calls=%fused_computation.37 | convolution fusion | flops 84542080 | bytes 18088256 | tf_op jit(solution)/shard_map/sn,nhde->shde/dot_general | solution.py:107
  (203 shorter events, 375.6 us)
Async XLA Ops:
  7.2 770.6 %all-gather.2.cloned.1.call-start = ((), (), s32[]{:S(2)}) async-start(), calls=%async_computation | async-start | bytes 17301504 | tf_op jit(solution)/shard_map/all_gather | solution.py:110
  277.4 10.7 %collective-permute-start = (f32[8,128,128]{2,1,0:T(8,128)S(1)}, f32[8,128,128]{2,1,0:T(8,128)S(1)}, u32[]{:S(2)}, u32[]{:S(2)}) collective-permute-start(f32[8,128,128]{2,1,0:T(8,128)S(1)} %multiply_add_fusion.2), channel_id=1, source_target_pairs={{0,4},{4,8},{8,12},{12,16},{16,20},{20,24},{24,28},{28,32},{32,36}... | collective-permute-start | bytes 1572872 | tf_op jit(solution)/shard_map/while/body/eval_jaxpr/ppermute | solution.py:14
  289.3 10.5 %collective-permute-start = (f32[8,128,128]{2,1,0:T(8,128)S(1)}, f32[8,128,128]{2,1,0:T(8,128)S(1)}, u32[]{:S(2)}, u32[]{:S(2)}) collective-permute-start(f32[8,128,128]{2,1,0:T(8,128)S(1)} %multiply_add_fusion.2), channel_id=1, source_target_pairs={{0,4},{4,8},{8,12},{12,16},{16,20},{20,24},{24,28},{28,32},{32,36}... | collective-permute-start | bytes 1572872 | tf_op jit(solution)/shard_map/while/body/eval_jaxpr/ppermute | solution.py:14
  300.9 10.5 %collective-permute-start = (f32[8,128,128]{2,1,0:T(8,128)S(1)}, f32[8,128,128]{2,1,0:T(8,128)S(1)}, u32[]{:S(2)}, u32[]{:S(2)}) collective-permute-start(f32[8,128,128]{2,1,0:T(8,128)S(1)} %multiply_add_fusion.2), channel_id=1, source_target_pairs={{0,4},{4,8},{8,12},{12,16},{16,20},{20,24},{24,28},{28,32},{32,36}... | collective-permute-start | bytes 1572872 | tf_op jit(solution)/shard_map/while/body/eval_jaxpr/ppermute | solution.py:14
  312.6 10.5 %collective-permute-start = (f32[8,128,128]{2,1,0:T(8,128)S(1)}, f32[8,128,128]{2,1,0:T(8,128)S(1)}, u32[]{:S(2)}, u32[]{:S(2)}) collective-permute-start(f32[8,128,128]{2,1,0:T(8,128)S(1)} %multiply_add_fusion.2), channel_id=1, source_target_pairs={{0,4},{4,8},{8,12},{12,16},{16,20},{20,24},{24,28},{28,32},{32,36}... | collective-permute-start | bytes 1572872 | tf_op jit(solution)/shard_map/while/body/eval_jaxpr/ppermute | solution.py:14
  324.3 10.5 %collective-permute-start = (f32[8,128,128]{2,1,0:T(8,128)S(1)}, f32[8,128,128]{2,1,0:T(8,128)S(1)}, u32[]{:S(2)}, u32[]{:S(2)}) collective-permute-start(f32[8,128,128]{2,1,0:T(8,128)S(1)} %multiply_add_fusion.2), channel_id=1, source_target_pairs={{0,4},{4,8},{8,12},{12,16},{16,20},{20,24},{24,28},{28,32},{32,36}... | collective-permute-start | bytes 1572872 | tf_op jit(solution)/shard_map/while/body/eval_jaxpr/ppermute | solution.py:14
  335.9 10.5 %collective-permute-start = (f32[8,128,128]{2,1,0:T(8,128)S(1)}, f32[8,128,128]{2,1,0:T(8,128)S(1)}, u32[]{:S(2)}, u32[]{:S(2)}) collective-permute-start(f32[8,128,128]{2,1,0:T(8,128)S(1)} %multiply_add_fusion.2), channel_id=1, source_target_pairs={{0,4},{4,8},{8,12},{12,16},{16,20},{20,24},{24,28},{28,32},{32,36}... | collective-permute-start | bytes 1572872 | tf_op jit(solution)/shard_map/while/body/eval_jaxpr/ppermute | solution.py:14
  347.6 10.5 %collective-permute-start = (f32[8,128,128]{2,1,0:T(8,128)S(1)}, f32[8,128,128]{2,1,0:T(8,128)S(1)}, u32[]{:S(2)}, u32[]{:S(2)}) collective-permute-start(f32[8,128,128]{2,1,0:T(8,128)S(1)} %multiply_add_fusion.2), channel_id=1, source_target_pairs={{0,4},{4,8},{8,12},{12,16},{16,20},{20,24},{24,28},{28,32},{32,36}... | collective-permute-start | bytes 1572872 | tf_op jit(solution)/shard_map/while/body/eval_jaxpr/ppermute | solution.py:14
  359.3 10.5 %collective-permute-start = (f32[8,128,128]{2,1,0:T(8,128)S(1)}, f32[8,128,128]{2,1,0:T(8,128)S(1)}, u32[]{:S(2)}, u32[]{:S(2)}) collective-permute-start(f32[8,128,128]{2,1,0:T(8,128)S(1)} %multiply_add_fusion.2), channel_id=1, source_target_pairs={{0,4},{4,8},{8,12},{12,16},{16,20},{20,24},{24,28},{28,32},{32,36}... | collective-permute-start | bytes 1572872 | tf_op jit(solution)/shard_map/while/body/eval_jaxpr/ppermute | solution.py:14
  370.9 10.5 %collective-permute-start = (f32[8,128,128]{2,1,0:T(8,128)S(1)}, f32[8,128,128]{2,1,0:T(8,128)S(1)}, u32[]{:S(2)}, u32[]{:S(2)}) collective-permute-start(f32[8,128,128]{2,1,0:T(8,128)S(1)} %multiply_add_fusion.2), channel_id=1, source_target_pairs={{0,4},{4,8},{8,12},{12,16},{16,20},{20,24},{24,28},{28,32},{32,36}... | collective-permute-start | bytes 1572872 | tf_op jit(solution)/shard_map/while/body/eval_jaxpr/ppermute | solution.py:14
  382.6 10.5 %collective-permute-start = (f32[8,128,128]{2,1,0:T(8,128)S(1)}, f32[8,128,128]{2,1,0:T(8,128)S(1)}, u32[]{:S(2)}, u32[]{:S(2)}) collective-permute-start(f32[8,128,128]{2,1,0:T(8,128)S(1)} %multiply_add_fusion.2), channel_id=1, source_target_pairs={{0,4},{4,8},{8,12},{12,16},{16,20},{20,24},{24,28},{28,32},{32,36}... | collective-permute-start | bytes 1572872 | tf_op jit(solution)/shard_map/while/body/eval_jaxpr/ppermute | solution.py:14
  394.3 10.5 %collective-permute-start = (f32[8,128,128]{2,1,0:T(8,128)S(1)}, f32[8,128,128]{2,1,0:T(8,128)S(1)}, u32[]{:S(2)}, u32[]{:S(2)}) collective-permute-start(f32[8,128,128]{2,1,0:T(8,128)S(1)} %multiply_add_fusion.2), channel_id=1, source_target_pairs={{0,4},{4,8},{8,12},{12,16},{16,20},{20,24},{24,28},{28,32},{32,36}... | collective-permute-start | bytes 1572872 | tf_op jit(solution)/shard_map/while/body/eval_jaxpr/ppermute | solution.py:14
  405.9 10.5 %collective-permute-start = (f32[8,128,128]{2,1,0:T(8,128)S(1)}, f32[8,128,128]{2,1,0:T(8,128)S(1)}, u32[]{:S(2)}, u32[]{:S(2)}) collective-permute-start(f32[8,128,128]{2,1,0:T(8,128)S(1)} %multiply_add_fusion.2), channel_id=1, source_target_pairs={{0,4},{4,8},{8,12},{12,16},{16,20},{20,24},{24,28},{28,32},{32,36}... | collective-permute-start | bytes 1572872 | tf_op jit(solution)/shard_map/while/body/eval_jaxpr/ppermute | solution.py:14
  417.6 10.5 %collective-permute-start = (f32[8,128,128]{2,1,0:T(8,128)S(1)}, f32[8,128,128]{2,1,0:T(8,128)S(1)}, u32[]{:S(2)}, u32[]{:S(2)}) collective-permute-start(f32[8,128,128]{2,1,0:T(8,128)S(1)} %multiply_add_fusion.2), channel_id=1, source_target_pairs={{0,4},{4,8},{8,12},{12,16},{16,20},{20,24},{24,28},{28,32},{32,36}... | collective-permute-start | bytes 1572872 | tf_op jit(solution)/shard_map/while/body/eval_jaxpr/ppermute | solution.py:14
  429.2 10.5 %collective-permute-start = (f32[8,128,128]{2,1,0:T(8,128)S(1)}, f32[8,128,128]{2,1,0:T(8,128)S(1)}, u32[]{:S(2)}, u32[]{:S(2)}) collective-permute-start(f32[8,128,128]{2,1,0:T(8,128)S(1)} %multiply_add_fusion.2), channel_id=1, source_target_pairs={{0,4},{4,8},{8,12},{12,16},{16,20},{20,24},{24,28},{28,32},{32,36}... | collective-permute-start | bytes 1572872 | tf_op jit(solution)/shard_map/while/body/eval_jaxpr/ppermute | solution.py:14
  440.9 10.5 %collective-permute-start = (f32[8,128,128]{2,1,0:T(8,128)S(1)}, f32[8,128,128]{2,1,0:T(8,128)S(1)}, u32[]{:S(2)}, u32[]{:S(2)}) collective-permute-start(f32[8,128,128]{2,1,0:T(8,128)S(1)} %multiply_add_fusion.2), channel_id=1, source_target_pairs={{0,4},{4,8},{8,12},{12,16},{16,20},{20,24},{24,28},{28,32},{32,36}... | collective-permute-start | bytes 1572872 | tf_op jit(solution)/shard_map/while/body/eval_jaxpr/ppermute | solution.py:14
  452.6 10.5 %collective-permute-start = (f32[8,128,128]{2,1,0:T(8,128)S(1)}, f32[8,128,128]{2,1,0:T(8,128)S(1)}, u32[]{:S(2)}, u32[]{:S(2)}) collective-permute-start(f32[8,128,128]{2,1,0:T(8,128)S(1)} %multiply_add_fusion.2), channel_id=1, source_target_pairs={{0,4},{4,8},{8,12},{12,16},{16,20},{20,24},{24,28},{28,32},{32,36}... | collective-permute-start | bytes 1572872 | tf_op jit(solution)/shard_map/while/body/eval_jaxpr/ppermute | solution.py:14
  464.2 10.5 %collective-permute-start = (f32[8,128,128]{2,1,0:T(8,128)S(1)}, f32[8,128,128]{2,1,0:T(8,128)S(1)}, u32[]{:S(2)}, u32[]{:S(2)}) collective-permute-start(f32[8,128,128]{2,1,0:T(8,128)S(1)} %multiply_add_fusion.2), channel_id=1, source_target_pairs={{0,4},{4,8},{8,12},{12,16},{16,20},{20,24},{24,28},{28,32},{32,36}... | collective-permute-start | bytes 1572872 | tf_op jit(solution)/shard_map/while/body/eval_jaxpr/ppermute | solution.py:14
  475.9 10.5 %collective-permute-start = (f32[8,128,128]{2,1,0:T(8,128)S(1)}, f32[8,128,128]{2,1,0:T(8,128)S(1)}, u32[]{:S(2)}, u32[]{:S(2)}) collective-permute-start(f32[8,128,128]{2,1,0:T(8,128)S(1)} %multiply_add_fusion.2), channel_id=1, source_target_pairs={{0,4},{4,8},{8,12},{12,16},{16,20},{20,24},{24,28},{28,32},{32,36}... | collective-permute-start | bytes 1572872 | tf_op jit(solution)/shard_map/while/body/eval_jaxpr/ppermute | solution.py:14
  487.6 11.5 %collective-permute-start = (f32[8,128,128]{2,1,0:T(8,128)S(1)}, f32[8,128,128]{2,1,0:T(8,128)S(1)}, u32[]{:S(2)}, u32[]{:S(2)}) collective-permute-start(f32[8,128,128]{2,1,0:T(8,128)S(1)} %multiply_add_fusion.2), channel_id=1, source_target_pairs={{0,4},{4,8},{8,12},{12,16},{16,20},{20,24},{24,28},{28,32},{32,36}... | collective-permute-start | bytes 1572872 | tf_op jit(solution)/shard_map/while/body/eval_jaxpr/ppermute | solution.py:14
  500.3 12.6 %collective-permute-start = (f32[8,128,128]{2,1,0:T(8,128)S(1)}, f32[8,128,128]{2,1,0:T(8,128)S(1)}, u32[]{:S(2)}, u32[]{:S(2)}) collective-permute-start(f32[8,128,128]{2,1,0:T(8,128)S(1)} %multiply_add_fusion.2), channel_id=1, source_target_pairs={{0,4},{4,8},{8,12},{12,16},{16,20},{20,24},{24,28},{28,32},{32,36}... | collective-permute-start | bytes 1572872 | tf_op jit(solution)/shard_map/while/body/eval_jaxpr/ppermute | solution.py:14
  514.0 12.6 %collective-permute-start = (f32[8,128,128]{2,1,0:T(8,128)S(1)}, f32[8,128,128]{2,1,0:T(8,128)S(1)}, u32[]{:S(2)}, u32[]{:S(2)}) collective-permute-start(f32[8,128,128]{2,1,0:T(8,128)S(1)} %multiply_add_fusion.2), channel_id=1, source_target_pairs={{0,4},{4,8},{8,12},{12,16},{16,20},{20,24},{24,28},{28,32},{32,36}... | collective-permute-start | bytes 1572872 | tf_op jit(solution)/shard_map/while/body/eval_jaxpr/ppermute | solution.py:14
  527.8 12.6 %collective-permute-start = (f32[8,128,128]{2,1,0:T(8,128)S(1)}, f32[8,128,128]{2,1,0:T(8,128)S(1)}, u32[]{:S(2)}, u32[]{:S(2)}) collective-permute-start(f32[8,128,128]{2,1,0:T(8,128)S(1)} %multiply_add_fusion.2), channel_id=1, source_target_pairs={{0,4},{4,8},{8,12},{12,16},{16,20},{20,24},{24,28},{28,32},{32,36}... | collective-permute-start | bytes 1572872 | tf_op jit(solution)/shard_map/while/body/eval_jaxpr/ppermute | solution.py:14
  541.6 12.6 %collective-permute-start = (f32[8,128,128]{2,1,0:T(8,128)S(1)}, f32[8,128,128]{2,1,0:T(8,128)S(1)}, u32[]{:S(2)}, u32[]{:S(2)}) collective-permute-start(f32[8,128,128]{2,1,0:T(8,128)S(1)} %multiply_add_fusion.2), channel_id=1, source_target_pairs={{0,4},{4,8},{8,12},{12,16},{16,20},{20,24},{24,28},{28,32},{32,36}... | collective-permute-start | bytes 1572872 | tf_op jit(solution)/shard_map/while/body/eval_jaxpr/ppermute | solution.py:14
  555.4 12.6 %collective-permute-start = (f32[8,128,128]{2,1,0:T(8,128)S(1)}, f32[8,128,128]{2,1,0:T(8,128)S(1)}, u32[]{:S(2)}, u32[]{:S(2)}) collective-permute-start(f32[8,128,128]{2,1,0:T(8,128)S(1)} %multiply_add_fusion.2), channel_id=1, source_target_pairs={{0,4},{4,8},{8,12},{12,16},{16,20},{20,24},{24,28},{28,32},{32,36}... | collective-permute-start | bytes 1572872 | tf_op jit(solution)/shard_map/while/body/eval_jaxpr/ppermute | solution.py:14
  569.1 12.6 %collective-permute-start = (f32[8,128,128]{2,1,0:T(8,128)S(1)}, f32[8,128,128]{2,1,0:T(8,128)S(1)}, u32[]{:S(2)}, u32[]{:S(2)}) collective-permute-start(f32[8,128,128]{2,1,0:T(8,128)S(1)} %multiply_add_fusion.2), channel_id=1, source_target_pairs={{0,4},{4,8},{8,12},{12,16},{16,20},{20,24},{24,28},{28,32},{32,36}... | collective-permute-start | bytes 1572872 | tf_op jit(solution)/shard_map/while/body/eval_jaxpr/ppermute | solution.py:14
  582.9 12.6 %collective-permute-start = (f32[8,128,128]{2,1,0:T(8,128)S(1)}, f32[8,128,128]{2,1,0:T(8,128)S(1)}, u32[]{:S(2)}, u32[]{:S(2)}) collective-permute-start(f32[8,128,128]{2,1,0:T(8,128)S(1)} %multiply_add_fusion.2), channel_id=1, source_target_pairs={{0,4},{4,8},{8,12},{12,16},{16,20},{20,24},{24,28},{28,32},{32,36}... | collective-permute-start | bytes 1572872 | tf_op jit(solution)/shard_map/while/body/eval_jaxpr/ppermute | solution.py:14
  596.7 12.6 %collective-permute-start = (f32[8,128,128]{2,1,0:T(8,128)S(1)}, f32[8,128,128]{2,1,0:T(8,128)S(1)}, u32[]{:S(2)}, u32[]{:S(2)}) collective-permute-start(f32[8,128,128]{2,1,0:T(8,128)S(1)} %multiply_add_fusion.2), channel_id=1, source_target_pairs={{0,4},{4,8},{8,12},{12,16},{16,20},{20,24},{24,28},{28,32},{32,36}... | collective-permute-start | bytes 1572872 | tf_op jit(solution)/shard_map/while/body/eval_jaxpr/ppermute | solution.py:14
  610.4 12.6 %collective-permute-start = (f32[8,128,128]{2,1,0:T(8,128)S(1)}, f32[8,128,128]{2,1,0:T(8,128)S(1)}, u32[]{:S(2)}, u32[]{:S(2)}) collective-permute-start(f32[8,128,128]{2,1,0:T(8,128)S(1)} %multiply_add_fusion.2), channel_id=1, source_target_pairs={{0,4},{4,8},{8,12},{12,16},{16,20},{20,24},{24,28},{28,32},{32,36}... | collective-permute-start | bytes 1572872 | tf_op jit(solution)/shard_map/while/body/eval_jaxpr/ppermute | solution.py:14
  624.2 12.6 %collective-permute-start = (f32[8,128,128]{2,1,0:T(8,128)S(1)}, f32[8,128,128]{2,1,0:T(8,128)S(1)}, u32[]{:S(2)}, u32[]{:S(2)}) collective-permute-start(f32[8,128,128]{2,1,0:T(8,128)S(1)} %multiply_add_fusion.2), channel_id=1, source_target_pairs={{0,4},{4,8},{8,12},{12,16},{16,20},{20,24},{24,28},{28,32},{32,36}... | collective-permute-start | bytes 1572872 | tf_op jit(solution)/shard_map/while/body/eval_jaxpr/ppermute | solution.py:14
  638.0 12.6 %collective-permute-start = (f32[8,128,128]{2,1,0:T(8,128)S(1)}, f32[8,128,128]{2,1,0:T(8,128)S(1)}, u32[]{:S(2)}, u32[]{:S(2)}) collective-permute-start(f32[8,128,128]{2,1,0:T(8,128)S(1)} %multiply_add_fusion.2), channel_id=1, source_target_pairs={{0,4},{4,8},{8,12},{12,16},{16,20},{20,24},{24,28},{28,32},{32,36}... | collective-permute-start | bytes 1572872 | tf_op jit(solution)/shard_map/while/body/eval_jaxpr/ppermute | solution.py:14
  651.8 12.6 %collective-permute-start = (f32[8,128,128]{2,1,0:T(8,128)S(1)}, f32[8,128,128]{2,1,0:T(8,128)S(1)}, u32[]{:S(2)}, u32[]{:S(2)}) collective-permute-start(f32[8,128,128]{2,1,0:T(8,128)S(1)} %multiply_add_fusion.2), channel_id=1, source_target_pairs={{0,4},{4,8},{8,12},{12,16},{16,20},{20,24},{24,28},{28,32},{32,36}... | collective-permute-start | bytes 1572872 | tf_op jit(solution)/shard_map/while/body/eval_jaxpr/ppermute | solution.py:14
  (18 other events, 505.2 us)
Sparse Core Ops, SparseCore 0:
  665.5 112.1 all-gather.1
where the time goes:
time: 808 us; the launch traced here: 801 us
  waiting for transfers between devices  255 us (32%)
  local copies, waits for them, and re-layouts  231 us (29%)
  starting transfers between devices  163 us (20%)
  matrix products  75.3 us (9%)
  other arithmetic  52.4 us (6%)
  between operations  14.2 us (2%)
  blocking collectives  9.83 us (1%)
    ppermute x31, waiting for transfers between devices, from_behind(): lax.ppermute(value, axis, [(source, source + steps) for source in range(f...  189 us
    dynamic_update_slice x8, local copies, waits for them, and re-layouts, shards(): lax.scan(local_step, zero_state, (query_blocks, key_blocks, value_blocks,...  178 us
    ppermute x31, starting transfers between devices, from_behind(): lax.ppermute(value, axis, [(source, source + steps) for source in range(f...  163 us
    all_gather x1, waiting for transfers between devices, shards(): lax.all_gather(snapshots, 'seq', axis=0, tiled=True)  65.4 us
    add x31, other arithmetic, combine(): jnp.exp(following[0])[:, None, None] * earlier[1] + following[1]  36.1 us
    dot_general x4, matrix products, block_terms(): jnp.einsum('hts,shd->thd', weights, value_blk, preferred_element_type=jnp...  20.8 us
    unnamed x25, local copies, waits for them, and re-layouts  20.6 us
  transfers between devices with their start and end apart: 32, of which 32 were waited for; matrix products, arithmetic and copies ran while one was open for 5% of the time, Pallas kernels for 0%

commit v1 on v0

v1 whole, which is shorter than its diff:
```python
import functools

import jax
import jax.numpy as jnp
from jax import lax
from jax.experimental import pallas as pl
from jax.experimental.pallas import tpu as pltpu
from jax.sharding import PartitionSpec as P

SLOTS = 5
HD = 128
HALF = 128
CHUNK = 256
LOG2E = 1.4426950408889634
BF = jnp.bfloat16
F32 = jnp.float32
MESH = pl.DeviceIdType.MESH
INTRA_EARLY = 4


def lanes_scan(x, lane):
    for shift in (1, 2, 4, 8, 16, 32, 64):
        x = x + jnp.where(lane >= shift, pltpu.roll(x, shift, axis=1), 0.0)
    return x


def three_parts(row, sub):
    x = jnp.broadcast_to(row, (8, 128))
    hi = x.astype(BF).astype(F32)
    rest = x - hi
    mid = rest.astype(BF).astype(F32)
    lo = rest - mid
    return jnp.where(sub == 0, hi, jnp.where(sub == 1, mid, jnp.where(sub == 2, lo, 0.0)))


def column_of(row):
    return jnp.broadcast_to(row, (HALF, HALF)).T


def kernel(
    n_seq,
    n_head,
    idx_ref,
    q_hbm,
    k_hbm,
    v_hbm,
    d_hbm,
    g_hbm,
    att_hbm,
    cache_hbm,
    qb,
    kb,
    vb,
    acc,
    ob,
    sl,
    up,
    en,
    d_ref,
    g_ref,
    c_ref,
    f_ref,
    a_ref,
    b_ref,
    pd_ref,
    sendbuf,
    recvbuf,
    snap,
    pagebuf,
    ent,
    sq_send,
    sq_recv,
    scale_ref,
    in_sem,
    q_sem,
    small_sem,
    a_send,
    a_recv,
    e_send,
    e_recv,
    p_send,
    p_recv,
    p_self,
    s_send,
    s_recv,
    o_sem,
):
    heads = kb.shape[0]
    toks = kb.shape[1]
    chunks = toks // CHUNK
    per_page = chunks // 2
    me = lax.axis_index("seq")
    z = lax.axis_index("head")
    parts = n_seq // heads
    rows = HD // parts
    g = me // parts
    r0 = pl.multiple_of((me % parts) * rows, rows)

    def kv_copies(step):
        h = (g + step) % heads
        hc = pl.multiple_of(h * HD, HD)
        return (
            pltpu.make_async_copy(k_hbm.at[:, pl.ds(hc, HD)], kb.at[h], in_sem.at[0, step]),
            pltpu.make_async_copy(v_hbm.at[:, pl.ds(hc, HD)], vb.at[h], in_sem.at[1, step]),
        )

    def q_copy(h):
        hc = pl.multiple_of(h * HD, HD)
        return pltpu.make_async_copy(q_hbm.at[:, pl.ds(hc, HD)], qb.at[h], q_sem.at[h])

    d_copy = pltpu.make_async_copy(d_hbm, d_ref, small_sem.at[0])
    g_copy = pltpu.make_async_copy(g_hbm, g_ref, small_sem.at[1])
    d_copy.start()

    @pl.loop(0, heads)
    def _(step):
        for copy in kv_copies(step):
            copy.start()

    @pl.loop(0, heads)
    def _(h):
        q_copy(h).start()

    g_copy.start()

    barrier = pltpu.get_barrier_semaphore()

    @pl.loop(1, n_seq)
    def _(step):
        pl.semaphore_signal(
            barrier, inc=1, device_id={"seq": (me + step) % n_seq}, device_id_type=MESH
        )

    @pl.loop(1, n_head)
    def _(step):
        pl.semaphore_signal(
            barrier, inc=1, device_id={"head": (z + step) % n_head}, device_id_type=MESH
        )

    d_copy.wait()
    lane = lax.broadcasted_iota(jnp.int32, (heads, 128), 1)
    start = None
    for n in range(chunks):
        lo = n * CHUNK
        x0 = lanes_scan(d_ref[:, lo : lo + HALF] * LOG2E, lane)
        x1 = lanes_scan(d_ref[:, lo + HALF : lo + CHUNK] * LOG2E, lane)
        x1 = x1 + jnp.broadcast_to(x0[:, 127:128], (heads, 128))
        last = jnp.broadcast_to(x1[:, 127:128], (heads, 128))
        factors = jnp.exp2(last)
        decays = jnp.exp2(last - x0), jnp.exp2(last - x1)
        if n % per_page == 0:
            start = jnp.zeros_like(last)
        begins = jnp.exp2(start)
        start = start + last
        pages = jnp.exp2(start)
        for h in range(heads):
            row = slice(h, h + 1)
            c_ref[h, :, lo : lo + HALF] = x0[row]
            c_ref[h, :, lo + HALF : lo + CHUNK] = x1[row]
            f_ref[h, :, lo : lo + HALF] = decays[0][row]
            f_ref[h, :, lo + HALF : lo + CHUNK] = decays[1][row]
            a_ref[h * chunks + n] = factors[row]
            b_ref[h * chunks + n] = begins[row]
            if n % per_page == per_page - 1:
                pd_ref[h * 2 + n // per_page] = pages[row]

    pl.semaphore_wait(barrier, n_seq - 1 + n_head - 1)

    sub = lax.broadcasted_iota(jnp.int32, (8, 128), 0)

    def send_slice(j):
        return pltpu.make_async_remote_copy(
            src_ref=sendbuf.at[j],
            dst_ref=recvbuf.at[me],
            send_sem=a_send,
            recv_sem=a_recv,
            device_id={"seq": j},
            device_id_type=MESH,
        )

    @pl.loop(0, heads)
    def _(step):
        h = (g + step) % heads
        for copy in kv_copies(step):
            copy.wait()
        ends = []
        state = None
        for n in range(chunks):
            lo = n * CHUNK
            kt = kb[h, lo : lo + CHUNK, :].T
            scaled = (kt.astype(F32) * f_ref[h, :, lo : lo + CHUNK]).astype(BF)
            update = jnp.dot(scaled, vb[h, lo : lo + CHUNK, :], preferred_element_type=F32)
            if n % per_page == 0:
                state = update
                sl[h * chunks + n] = jnp.zeros_like(update)
            else:
                sl[h * chunks + n] = state
                state = a_ref[h * chunks + n] * state + update
            if n % per_page == per_page - 1:
                ends.append(state)
        up[h] = ends[0]
        decays = jnp.concatenate(
            [
                three_parts(pd_ref[2 * h], sub),
                three_parts(pd_ref[2 * h + 1], sub),
            ],
            axis=0,
        ).astype(BF)
        for part in range(parts):
            j = h * parts + part
            first = ends[0][part * rows : (part + 1) * rows].astype(BF)
            second = ends[1][part * rows : (part + 1) * rows].astype(BF)

            @pl.when(j != me)
            def _():
                sendbuf[j, 0:rows] = first
                sendbuf[j, rows : 2 * rows] = second
                sendbuf[j, 2 * rows : 2 * rows + 16] = decays
                send_slice(j).start()

            @pl.when(j == me)
            def _():
                recvbuf[me, 0:rows] = first
                recvbuf[me, rows : 2 * rows] = second
                recvbuf[me, 2 * rows : 2 * rows + 16] = decays

    tri = lax.broadcasted_iota(jnp.int32, (HALF, HALF), 0) >= lax.broadcasted_iota(
        jnp.int32, (HALF, HALF), 1
    )

    def intra(h):
        q_copy(h).wait()
        for n in range(chunks):
            lo = n * CHUNK
            q = qb[h, lo : lo + CHUNK, :]
            k = kb[h, lo : lo + CHUNK, :]
            row0 = c_ref[h, :, lo : lo + HALF]
            row1 = c_ref[h, :, lo + HALF : lo + CHUNK]
            col0, col1 = column_of(row0), column_of(row1)
            scores = lax.dot_general(
                q, k, (((1,), (1,)), ((), ())), preferred_element_type=F32
            )
            w00 = scores[:HALF, :HALF] * jnp.exp2(jnp.where(tri, col0 - row0, -1e30))
            w10 = scores[HALF:, :HALF] * jnp.exp2(col1 - row0)
            w11 = scores[HALF:, HALF:] * jnp.exp2(jnp.where(tri, col1 - row1, -1e30))
            acc[h, lo : lo + HALF, :] = jnp.dot(
                w00.astype(BF), vb[h, lo : lo + HALF, :], preferred_element_type=F32
            )
            acc[h, lo + HALF : lo + CHUNK, :] = jnp.dot(
                jnp.concatenate([w10.astype(BF), w11.astype(BF)], axis=1),
                vb[h, lo : lo + CHUNK, :],
                preferred_element_type=F32,
            )
            qb[h, lo : lo + HALF, :] = (q[:HALF].astype(F32) * jnp.exp2(col0)).astype(BF)
            qb[h, lo + HALF : lo + CHUNK, :] = (q[HALF:].astype(F32) * jnp.exp2(col1)).astype(BF)

    pl.loop(0, INTRA_EARLY)(intra)

    pltpu.make_async_copy(
        recvbuf.at[pl.ds(0, n_seq - 1)], recvbuf.at[pl.ds(0, n_seq - 1)], a_recv
    ).wait()
    snap[0] = jnp.zeros((rows, HD), BF)

    def pages_of(i, state):
        decays = recvbuf[i, 2 * rows : 2 * rows + 16].astype(F32)
        a0 = decays[0:1] + decays[1:2] + decays[2:3]
        a1 = decays[8:9] + decays[9:10] + decays[10:11]
        state = a0 * state + recvbuf[i, 0:rows].astype(F32)
        snap[2 * i + 1] = state.astype(BF)
        state = a1 * state + recvbuf[i, rows : 2 * rows].astype(F32)
        snap[2 * i + 2] = state.astype(BF)
        return state

    lax.fori_loop(0, n_seq, pages_of, jnp.zeros((rows, HD), F32), unroll=4)

    def send_entry(i):
        return pltpu.make_async_remote_copy(
            src_ref=snap.at[2 * i],
            dst_ref=ent.at[g, pl.ds(r0, rows), :],
            send_sem=e_send,
            recv_sem=e_recv,
            device_id={"seq": i},
            device_id_type=MESH,
        )

    @pl.loop(1, n_seq)
    def _(step):
        send_entry((me + step) % n_seq).start()

    ent[g, pl.ds(r0, rows), :] = snap[2 * me]

    def send_pages(i):
        return pltpu.make_async_remote_copy(
            src_ref=pagebuf.at[pl.ds(i * SLOTS, SLOTS)],
            dst_ref=cache_hbm.at[:, g, pl.ds(r0, rows), :],
            send_sem=p_send,
            recv_sem=p_recv,
            device_id={"seq": i},
            device_id_type=MESH,
        )

    own_pages = pltpu.make_async_copy(
        pagebuf.at[pl.ds(me * SLOTS, SLOTS)], cache_hbm.at[:, g, pl.ds(r0, rows), :], p_self
    )

    def fill(i):
        for s in range(SLOTS):
            pagebuf[i * SLOTS + s] = snap[idx_ref[i * SLOTS + s]]

    @pl.loop(1, n_seq)
    def _(step):
        i = (me + step) % n_seq
        fill(i)
        send_pages(i).start()

    fill(me)
    own_pages.start()

    pl.loop(INTRA_EARLY, heads)(intra)

    pltpu.make_async_copy(
        snap.at[pl.ds(0, n_seq - 1)], snap.at[pl.ds(0, n_seq - 1)], e_recv
    ).wait()

    @pl.loop(0, heads)
    def _(h):
        en[h] = ent[h].astype(F32)
        en[heads + h] = pd_ref[2 * h] * ent[h].astype(F32) + up[h]

    def send_squares(half, step):
        return pltpu.make_async_remote_copy(
            src_ref=sq_send.at[half],
            dst_ref=sq_recv.at[half, step - 1],
            send_sem=s_send.at[half],
            recv_sem=s_recv.at[half],
            device_id={"head": (z + step) % n_head},
            device_id_type=MESH,
        )

    def finish(half):
        @pl.loop(0, per_page)
        def _(m):
            n = half * per_page + m
            lo = pl.multiple_of(n * CHUNK, CHUNK)
            squares = None
            for h in range(heads):
                state = (
                    sl[h * chunks + n] + b_ref[h * chunks + n] * en[half * heads + h]
                ).astype(BF)
                out = acc[h, pl.ds(lo, CHUNK), :] + jnp.dot(
                    qb[h, pl.ds(lo, CHUNK), :], state, preferred_element_type=F32
                )
                acc[h, pl.ds(lo, CHUNK), :] = out
                squares = out * out if squares is None else squares + out * out
            sq_send[half, 2 * m] = jnp.sum(squares[:HALF].T, axis=0, keepdims=True)
            sq_send[half, 2 * m + 1] = jnp.sum(squares[HALF:].T, axis=0, keepdims=True)

        for step in range(1, n_head):
            send_squares(half, step).start()

    def out_copy(n):
        lo = pl.multiple_of(n * CHUNK, CHUNK)
        return pltpu.make_async_copy(
            ob.at[pl.ds(lo, CHUNK), :], att_hbm.at[pl.ds(lo, CHUNK), :], o_sem
        )

    def normalize(half):
        received = sq_recv.at[half]
        pltpu.make_async_copy(received, received, s_recv.at[half]).wait()
        total = sq_send[half]
        for step in range(n_head - 1):
            total = total + sq_recv[half, step]
        scale_ref[...] = lax.rsqrt(total / (heads * HD * n_head) + 1e-6)

        @pl.loop(0, per_page)
        def _(m):
            n = half * per_page + m
            lo = pl.multiple_of(n * CHUNK, CHUNK)
            for side in range(2):
                scale = column_of(scale_ref[2 * m + side])
                at = pl.ds(pl.multiple_of(lo + side * HALF, HALF), HALF)
                for h in range(heads):
                    ob[at, h * HD : (h + 1) * HD] = (
                        acc[h, at, :] * scale * g_ref[h : h + 1, :]
                    ).astype(BF)
            out_copy(n).start()

    finish(0)
    finish(1)
    g_copy.wait()
    normalize(0)
    normalize(1)

    pltpu.make_async_copy(ob, att_hbm, o_sem).wait()
    own_pages.wait()
    sent = sendbuf.at[pl.ds(0, n_seq - 1)]
    pltpu.make_async_copy(sent, sent, a_send).wait()
    entries = snap.at[pl.ds(0, n_seq - 1)]
    pltpu.make_async_copy(entries, entries, e_send).wait()
    for half in range(2):
        received = sq_recv.at[half]
        pltpu.make_async_copy(received, received, s_send.at[half]).wait()
    pages = pagebuf.at[pl.ds(0, (n_seq - 1) * SLOTS)]
    pltpu.make_async_copy(pages, pages, p_send).wait()
    pltpu.make_async_copy(pages, pages, p_recv).wait()


def shards(n_seq, n_head, queries, key_rows, value_rows, decay_log, norm_gain, page_owner):
    toks, width = queries.shape
    heads = decay_log.shape[0]
    chunks = toks // CHUNK
    rows = HD * heads // n_seq
    n_pages = page_owner.shape[0]
    order = jnp.arange(n_pages, dtype=jnp.int32)
    earlier = (page_owner[:, None] == page_owner[None, :]) & (order[:, None] < order[None, :])
    slot = jnp.sum(earlier.astype(jnp.int32), axis=0)
    target = page_owner * SLOTS + slot
    wanted = target[None, :] == jnp.arange(n_seq * SLOTS, dtype=jnp.int32)[:, None]
    index = jnp.sum(jnp.where(wanted, order[None, :] + 1, 0), axis=1).astype(jnp.int32)
    anywhere = pl.BlockSpec(memory_space=pl.ANY)
    dma = pltpu.SemaphoreType.DMA
    return pl.pallas_call(
        functools.partial(kernel, n_seq, n_head),
        out_shape=(
            jax.ShapeDtypeStruct((toks, width), BF),
            jax.ShapeDtypeStruct((SLOTS, heads, HD, HD), BF),
        ),
        in_specs=[pl.BlockSpec(memory_space=pltpu.SMEM)] + [anywhere] * 5,
        out_specs=(anywhere, anywhere),
        scratch_shapes=[
            pltpu.VMEM((heads, toks, HD), BF),
            pltpu.VMEM((heads, toks, HD), BF),
            pltpu.VMEM((heads, toks, HD), BF),
            pltpu.VMEM((heads, toks, HD), F32),
            pltpu.VMEM((toks, width), BF),
            pltpu.VMEM((heads * chunks, HD, HD), F32),
            pltpu.VMEM((heads, HD, HD), F32),
            pltpu.VMEM((2 * heads, HD, HD), F32),
            pltpu.VMEM((heads, toks), F32),
            pltpu.VMEM((heads, HD), F32),
            pltpu.VMEM((heads, 1, toks), F32),
            pltpu.VMEM((heads, 1, toks), F32),
            pltpu.VMEM((heads * chunks, 1, 128), F32),
            pltpu.VMEM((heads * chunks, 1, 128), F32),
            pltpu.VMEM((heads * 2, 1, 128), F32),
            pltpu.VMEM((n_seq, 2 * rows + 16, HD), BF),
            pltpu.VMEM((n_seq, 2 * rows + 16, HD), BF),
            pltpu.VMEM((n_pages + 1, rows, HD), BF),
            pltpu.VMEM((n_seq * SLOTS, rows, HD), BF),
            pltpu.VMEM((heads, HD, HD), BF),
            pltpu.VMEM((2, 8, 1, 128), F32),
            pltpu.VMEM((2, n_head - 1, 8, 1, 128), F32),
            pltpu.VMEM((8, 1, 128), F32),
            dma((2, heads)),
            dma((heads,)),
            dma((2,)),
            dma,
            dma,
            dma,
            dma,
            dma,
            dma,
            dma,
            dma((2,)),
            dma((2,)),
            dma,
        ],
        compiler_params=pltpu.CompilerParams(
            collective_id=0, has_side_effects=True, vmem_limit_bytes=48 * 1024 * 1024
        ),
    )(
        index,
        queries,
        key_rows,
        value_rows,
        decay_log,
        norm_gain.reshape(heads, HD),
    )


def solution(mesh):
    return jax.shard_map(
        functools.partial(shards, mesh.shape["seq"], mesh.shape["head"]),
        mesh=mesh,
        in_specs=(
            P("seq", "head"),
            P("seq", "head"),
            P("seq", "head"),
            P("head", "seq"),
            P("head"),
            P(),
        ),
        out_specs=(P("seq", "head"), P("seq", "head", None, None)),
        check_vma=False,
    )
```

time: 808 us -> 53.4 us (0.07)
  the two profiles are of different devices: /device:TPU:1 before, /device:TPU:6 now
where the time goes in v1:
time: 53.4 us; the launch traced here: 53.2 us
  Pallas kernels  46.4 us (87%)
  local copies, waits for them, and re-layouts  4.59 us (9%)
  other arithmetic  1.58 us (3%)
  between operations  0.65 us (1%)
    pallas_call x1, Pallas kernels, shards(): pl.pallas_call(functools.partial(kernel, n_seq, n_head), out_shape=(jax.S...  46.4 us
    unnamed x6, local copies, waits for them, and re-layouts  4.59 us

profile of v1, /device:TPU:6, one launch (start us, length us, event | category | flops | bytes accessed | tf_op | source)
XLA Modules:
  0.0 53.2 jit_solution(1287197141225589930)
XLA Ops:
  0.6 0.8 %convert_reduce_fusion = s32[64]{0:T(128)S(1)} fusion(s32[64]{0:T(128)} %param.11), kind=kLoop, calls=%fused_computation.2 | loop fusion | flops 20416 | bytes 512 | tf_op jit(solution)/shard_map/reduce_sum | solution.py:416
  1.5 0.7 %iota_add_fusion = (s32[64]{0:T(128)S(1)}, s32[64]{0:T(128)S(1)}) fusion(s32[64]{0:T(128)S(1)} %convert_reduce_fusion, s32[64]{0:T(128)} %param.11), kind=kLoop, calls=%fused_computation.5 | loop fusion | flops 192 | bytes 1024 | tf_op jit(solution)/shard_map/add | solution.py:419
  2.1 0.1 select_reduce_fusion.idx_ref
  2.2 0.0 copy-start
  2.2 0.8 %copy-done = f32[8,2048]{1,0:T(8,128)S(1)} copy-done((f32[8,2048]{1,0:T(8,128)S(1)}, f32[8,2048]{1,0:T(8,128)}, u32[]{:S(2)}) %copy-start) | copy-done | bytes 65560
  3.1 0.0 copy-start.1
  3.1 0.7 %copy-done.1 = f32[1024]{0:T(1024)S(1)} copy-done((f32[1024]{0:T(1024)S(1)}, f32[1024]{0:T(1024)}, u32[]{:S(2)}) %copy-start.1) | copy-done | bytes 4120
  3.7 46.4 %shard_map.77 = (bf16[2048,1024]{1,0:T(8,128)(2,1)S(1)}, bf16[5,8,128,128]{3,2,1,0:T(8,128)(2,1)S(1)}) custom-call(s32[160]{0:T(256)S(1)} %select_reduce_fusion.idx_ref, bf16[2048,1024]{1,0:T(8,128)(2,1)} %q_hbm.1, bf16[2048,1024]{1,0:T(8,128)(2,1)} %k_hbm.1, bf16[2048,1024]{1,0:T(8,128)(2,1)} %v_hbm.1, f32[8,2048]{1,0:T(8,128)S(1)} %copy-done, ...), custom_call_target="tpu_custom_call" | custom-call | tf_op jit(solution)/shard_map/pallas_call | solution.py:422
  50.2 2.0 %copy.10 = bf16[2048,1024]{1,0:T(8,128)(2,1)} copy(bf16[2048,1024]{1,0:T(8,128)(2,1)S(1)} %get-tuple-element.6) | data formatting | bytes 8388608
  52.2 1.1 %copy.11 = bf16[5,8,128,128]{3,2,1,0:T(8,128)(2,1)} copy(bf16[5,8,128,128]{3,2,1,0:T(8,128)(2,1)S(1)} %get-tuple-element.7) | data formatting | bytes 2621440
Async XLA Ops:
  2.2 0.8 %copy-start = (f32[8,2048]{1,0:T(8,128)S(1)}, f32[8,2048]{1,0:T(8,128)}, u32[]{:S(2)}) copy-start(f32[8,2048]{1,0:T(8,128)} %d_hbm.1) | copy-start | bytes 196612
  3.1 0.7 %copy-start.1 = (f32[1024]{0:T(1024)S(1)}, f32[1024]{0:T(1024)}, u32[]{:S(2)}) copy-start(f32[1024]{0:T(1024)} %param.10) | copy-start | bytes 12292

commit v2 on v1

v2 whole, which is shorter than its diff:
```python
import functools

import jax
import jax.numpy as jnp
from jax import lax
from jax.experimental import pallas as pl
from jax.experimental.pallas import tpu as pltpu
from jax.sharding import PartitionSpec as P

SLOTS = 5
HD = 128
HALF = 128
CHUNK = 256
LOG2E = 1.4426950408889634
BF = jnp.bfloat16
F32 = jnp.float32
MESH = pl.DeviceIdType.MESH
FIRST = 1
SECOND = 3
STAGES = 2


def lanes_scan(x, lane):
    for shift in (1, 2, 4, 8, 16, 32, 64):
        x = x + jnp.where(lane >= shift, pltpu.roll(x, shift, axis=1), 0.0)
    return x


def far_first(a):
    return 2 + a - lax.div(a, 2) * (2 * a - 1)


def column_of(row):
    return jnp.broadcast_to(row, (HALF, HALF)).T


def kernel(
    n_seq,
    n_head,
    idx_ref,
    q_hbm,
    k_hbm,
    v_hbm,
    d_hbm,
    g_hbm,
    att_hbm,
    cache_hbm,
    qb,
    kb,
    vb,
    acc,
    ec,
    ob,
    sl,
    d_ref,
    g_ref,
    c_ref,
    f_ref,
    a_ref,
    b_ref,
    b2_ref,
    pd_ref,
    dec_recv,
    sendbuf,
    recvbuf,
    snap,
    pagebuf,
    ent,
    sq_send,
    sq_recv,
    scale_ref,
    in_sem,
    q_sem,
    small_sem,
    d_send,
    d_recv,
    a_send,
    a_recv,
    e_send,
    e_recv,
    p_send,
    p_recv,
    p_self,
    s_send,
    s_recv,
    o_sem,
):
    heads, toks = kb.shape[0], kb.shape[1]
    chunks = toks // CHUNK
    per_page = chunks // 2
    classes = heads // STAGES
    parts = n_seq // classes
    rows = HD // parts
    me = lax.axis_index("seq")
    z = lax.axis_index("head")
    x, y, core = lax.div(me, 8), lax.rem(lax.div(me, 2), 4), lax.rem(me, 2)
    mine = lax.rem(x + y, classes)
    r0 = pl.multiple_of((x * 2 + core) * rows, rows)

    steps = (2, 1, 3, 0)
    at_y = [lax.rem(y + d, 4) * 2 for d in steps]
    at_core = [1 - core, core]

    def each_other(visit):
        @pl.loop(0, 4)
        def _(a):
            at_x = lax.rem(x + far_first(a), 4) * 8
            for i in range(4):
                for k in range(2):
                    j = at_x + at_y[i] + at_core[k]
                    if i == 3 and k == 1:
                        pl.when(a < 3)(functools.partial(visit, j))
                    else:
                        visit(j)

    def class_of(j):
        return lax.rem(lax.div(j, 8) + lax.rem(lax.div(j, 2), 4), classes)

    def keeper(cls, px, pc):
        return (px * 4 + lax.rem(cls + 4 - px, 4)) * 2 + pc

    def class_at(s):
        return lax.rem(mine + far_first(s), classes)

    def kv_copies(stage, s):
        h = stage * classes + class_at(s)
        hc = pl.multiple_of(h * HD, HD)
        at = stage * classes + s
        return (
            pltpu.make_async_copy(k_hbm.at[:, pl.ds(hc, HD)], kb.at[h], in_sem.at[0, at]),
            pltpu.make_async_copy(v_hbm.at[:, pl.ds(hc, HD)], vb.at[h], in_sem.at[1, at]),
        )

    def q_copy(h):
        hc = pl.multiple_of(h * HD, HD)
        return pltpu.make_async_copy(q_hbm.at[:, pl.ds(hc, HD)], qb.at[h], q_sem.at[h])

    d_copy = pltpu.make_async_copy(d_hbm, d_ref, small_sem.at[0])
    g_copy = pltpu.make_async_copy(g_hbm, g_ref, small_sem.at[1])
    d_copy.start()
    for stage in range(STAGES):

        @pl.loop(0, classes)
        def _(s):
            for copy in kv_copies(stage, s):
                copy.start()

    barrier = pltpu.get_barrier_semaphore()

    each_other(
        lambda j: pl.semaphore_signal(
            barrier, inc=1, device_id={"seq": j}, device_id_type=MESH
        )
    )
    for step in range(1, n_head):
        pl.semaphore_signal(
            barrier, inc=1, device_id={"head": lax.rem(z + step, n_head)}, device_id_type=MESH
        )

    d_copy.wait()
    lane = lax.broadcasted_iota(jnp.int32, (heads, 128), 1)
    start = whole = None
    for n in range(chunks):
        lo = n * CHUNK
        x0 = lanes_scan(d_ref[:, lo : lo + HALF] * LOG2E, lane)
        x1 = lanes_scan(d_ref[:, lo + HALF : lo + CHUNK] * LOG2E, lane)
        x1 = x1 + jnp.broadcast_to(x0[:, 127:128], (heads, 128))
        last = jnp.broadcast_to(x1[:, 127:128], (heads, 128))
        factors = jnp.exp2(last)
        decays = jnp.exp2(last - x0), jnp.exp2(last - x1)
        if n == 0:
            whole = jnp.zeros_like(last)
        if n % per_page == 0:
            start = jnp.zeros_like(last)
        begins, begins2 = jnp.exp2(start), jnp.exp2(whole)
        start, whole = start + last, whole + last
        pages = jnp.exp2(start)
        for h in range(heads):
            row = slice(h, h + 1)
            c_ref[h, :, lo : lo + HALF] = x0[row]
            c_ref[h, :, lo + HALF : lo + CHUNK] = x1[row]
            f_ref[h, :, lo : lo + HALF] = decays[0][row]
            f_ref[h, :, lo + HALF : lo + CHUNK] = decays[1][row]
            a_ref[h * chunks + n] = factors[row]
            b_ref[h * chunks + n] = begins[row]
            b2_ref[h * chunks + n] = begins2[row]
            if n % per_page == per_page - 1:
                pd_ref[h % classes, h // classes, n // per_page] = pages[row]

    def send_decays(j):
        return pltpu.make_async_remote_copy(
            src_ref=pd_ref.at[class_of(j)],
            dst_ref=dec_recv.at[me],
            send_sem=d_send,
            recv_sem=d_recv,
            device_id={"seq": j},
            device_id_type=MESH,
        )

    dec_recv[me] = pd_ref[mine]

    def send_rows(stage, j):
        return pltpu.make_async_remote_copy(
            src_ref=sendbuf.at[stage, j],
            dst_ref=recvbuf.at[stage, me],
            send_sem=a_send.at[stage],
            recv_sem=a_recv.at[stage],
            device_id={"seq": j},
            device_id_type=MESH,
        )

    def send_class(stage, cls):
        @pl.loop(0, 4)
        def _(a):
            for side in range(2):
                j = keeper(cls, lax.rem(x + far_first(a), 4), side)

                @pl.when(j != me)
                def _():
                    send_rows(stage, j).start()

                @pl.when(j == me)
                def _():
                    recvbuf[stage, me] = sendbuf[stage, me]

    def states(stage):
        @pl.loop(0, classes)
        def _(s):
            cls = class_at(s)
            h = stage * classes + cls
            for copy in kv_copies(stage, s):
                copy.wait()
            ends = []
            state = None
            for n in range(chunks):
                lo = n * CHUNK
                kt = kb[h, lo : lo + CHUNK, :].T
                scaled = (kt.astype(F32) * f_ref[h, :, lo : lo + CHUNK]).astype(BF)
                update = jnp.dot(scaled, vb[h, lo : lo + CHUNK, :], preferred_element_type=F32)
                if n == 0:
                    sl[h * chunks] = jnp.zeros_like(update, BF)
                elif n < per_page:
                    sl[h * chunks + n] = state.astype(BF)
                elif n == per_page:
                    sl[h * chunks + n] = ends[0].astype(BF)
                else:
                    sl[h * chunks + n] = (state + b_ref[h * chunks + n] * ends[0]).astype(BF)
                state = update if n % per_page == 0 else a_ref[h * chunks + n] * state + update
                if n % per_page == per_page - 1:
                    ends.append(state)
            for part in range(parts):
                j = keeper(cls, part // 2, part % 2)
                for page in range(2):
                    sendbuf[stage, j, page] = ends[page][part * rows : (part + 1) * rows].astype(BF)

            if stage > 0:
                send_class(stage, cls)

    tri = lax.broadcasted_iota(jnp.int32, (HALF, HALF), 0) >= lax.broadcasted_iota(
        jnp.int32, (HALF, HALF), 1
    )

    def intra(h):
        q_copy(h).wait()
        for n in range(chunks):
            lo = n * CHUNK
            q = qb[h, lo : lo + CHUNK, :]
            k = kb[h, lo : lo + CHUNK, :]
            row0 = c_ref[h, :, lo : lo + HALF]
            row1 = c_ref[h, :, lo + HALF : lo + CHUNK]
            col0, col1 = column_of(row0), column_of(row1)
            scores = lax.dot_general(
                q, k, (((1,), (1,)), ((), ())), preferred_element_type=F32
            )
            w00 = scores[:HALF, :HALF] * jnp.exp2(jnp.where(tri, col0 - row0, -1e30))
            w10 = scores[HALF:, :HALF] * jnp.exp2(col1 - row0)
            w11 = scores[HALF:, HALF:] * jnp.exp2(jnp.where(tri, col1 - row1, -1e30))
            out0 = jnp.dot(w00.astype(BF), vb[h, lo : lo + HALF, :], preferred_element_type=F32)
            out1 = jnp.dot(
                jnp.concatenate([w10.astype(BF), w11.astype(BF)], axis=1),
                vb[h, lo : lo + CHUNK, :],
                preferred_element_type=F32,
            )
            e0, e1 = jnp.exp2(col0), jnp.exp2(col1)
            if n > 0:
                carried = jnp.dot(q, sl[h * chunks + n], preferred_element_type=F32)
                out0 = out0 + e0 * carried[:HALF]
                out1 = out1 + e1 * carried[HALF:]
            acc[h, lo : lo + HALF, :] = out0
            acc[h, lo + HALF : lo + CHUNK, :] = out1
            ec[h, lo : lo + HALF, :] = e0
            ec[h, lo + HALF : lo + CHUNK, :] = e1

    def wait_rows(stage):
        arrived = recvbuf.at[stage, pl.ds(0, n_seq - 1)]
        pltpu.make_async_copy(arrived, arrived, a_recv.at[stage]).wait()

    def recur(stage):
        snap[0, stage] = jnp.zeros((rows, HD), BF)

        def pages_of(i, state):
            state = dec_recv[i, stage, 0] * state + recvbuf[stage, i, 0].astype(F32)
            snap[2 * i + 1, stage] = state.astype(BF)
            state = dec_recv[i, stage, 1] * state + recvbuf[stage, i, 1].astype(F32)
            snap[2 * i + 2, stage] = state.astype(BF)
            return state

        lax.fori_loop(0, n_seq, pages_of, jnp.zeros((rows, HD), F32), unroll=8)

    def send_entry(i):
        return pltpu.make_async_remote_copy(
            src_ref=snap.at[2 * i],
            dst_ref=ent.at[:, mine, pl.ds(r0, rows), :],
            send_sem=e_send,
            recv_sem=e_recv,
            device_id={"seq": i},
            device_id_type=MESH,
        )

    def kept(stage):
        return cache_hbm.at[:, stage * classes + mine, pl.ds(r0, rows), :]

    def send_pages(stage, i):
        return pltpu.make_async_remote_copy(
            src_ref=pagebuf.at[stage, pl.ds(i * SLOTS, SLOTS)],
            dst_ref=kept(stage),
            send_sem=p_send.at[stage],
            recv_sem=p_recv.at[stage],
            device_id={"seq": i},
            device_id_type=MESH,
        )

    def own_pages(stage):
        return pltpu.make_async_copy(
            pagebuf.at[stage, pl.ds(me * SLOTS, SLOTS)], kept(stage), p_self.at[stage]
        )

    def hand_out(stage):
        def fill(i):
            for s in range(SLOTS):
                pagebuf[stage, i * SLOTS + s] = snap[idx_ref[i * SLOTS + s], stage]

        def visit(i):
            fill(i)
            send_pages(stage, i).start()

        each_other(visit)
        fill(me)
        own_pages(stage).start()

    states(0)
    pl.semaphore_wait(barrier, n_seq - 1 + n_head - 1)
    each_other(lambda j: send_decays(j).start())
    each_other(lambda j: send_rows(0, j).start())
    recvbuf[0, me] = sendbuf[0, me]

    @pl.loop(0, heads)
    def _(h):
        q_copy(h).start()

    g_copy.start()
    states(1)
    pl.loop(0, FIRST)(intra)
    all_decays = dec_recv.at[pl.ds(0, n_seq - 1)]
    pltpu.make_async_copy(all_decays, all_decays, d_recv).wait()
    wait_rows(0)
    recur(0)
    hand_out(0)
    pl.loop(FIRST, SECOND)(intra)
    wait_rows(1)
    recur(1)
    each_other(lambda i: send_entry(i).start())
    ent[:, mine, pl.ds(r0, rows), :] = snap[2 * me]

    hand_out(1)
    pl.loop(SECOND, heads)(intra)

    entries = snap.at[pl.ds(0, n_seq - 1)]
    pltpu.make_async_copy(entries, entries, e_recv).wait()

    def send_squares(half, step):
        return pltpu.make_async_remote_copy(
            src_ref=sq_send.at[half],
            dst_ref=sq_recv.at[half, step - 1],
            send_sem=s_send.at[half],
            recv_sem=s_recv.at[half],
            device_id={"head": lax.rem(z + step, n_head)},
            device_id_type=MESH,
        )

    def finish(half):
        @pl.loop(0, per_page)
        def _(m):
            n = half * per_page + m
            lo = pl.multiple_of(n * CHUNK, CHUNK)
            squares = None
            for h in range(heads):
                carried = jnp.dot(
                    qb[h, pl.ds(lo, CHUNK), :],
                    ent[h // classes, h % classes],
                    preferred_element_type=F32,
                )
                scale = ec[h, pl.ds(lo, CHUNK), :] * b2_ref[h * chunks + n]
                out = acc[h, pl.ds(lo, CHUNK), :] + scale * carried
                acc[h, pl.ds(lo, CHUNK), :] = out
                squares = out * out if squares is None else squares + out * out
            sq_send[half, 2 * m] = jnp.sum(squares[:HALF].T, axis=0, keepdims=True)
            sq_send[half, 2 * m + 1] = jnp.sum(squares[HALF:].T, axis=0, keepdims=True)

        for step in range(1, n_head):
            send_squares(half, step).start()

    def out_copy(n):
        lo = pl.multiple_of(n * CHUNK, CHUNK)
        return pltpu.make_async_copy(
            ob.at[pl.ds(lo, CHUNK), :], att_hbm.at[pl.ds(lo, CHUNK), :], o_sem
        )

    def normalize(half):
        received = sq_recv.at[half]
        pltpu.make_async_copy(received, received, s_recv.at[half]).wait()
        total = sq_send[half]
        for step in range(n_head - 1):
            total = total + sq_recv[half, step]
        scale_ref[...] = lax.rsqrt(total / (heads * HD * n_head) + 1e-6)

        @pl.loop(0, per_page)
        def _(m):
            n = half * per_page + m
            lo = pl.multiple_of(n * CHUNK, CHUNK)
            for side in range(2):
                scale = column_of(scale_ref[2 * m + side])
                at = pl.ds(pl.multiple_of(lo + side * HALF, HALF), HALF)
                for h in range(heads):
                    ob[at, h * HD : (h + 1) * HD] = (
                        acc[h, at, :] * scale * g_ref[h : h + 1, :]
                    ).astype(BF)
            out_copy(n).start()

    finish(0)
    finish(1)
    g_copy.wait()
    normalize(0)
    normalize(1)

    pltpu.make_async_copy(entries, entries, e_send).wait()
    pltpu.make_async_copy(ob, att_hbm, o_sem).wait()
    pltpu.make_async_copy(all_decays, all_decays, d_send).wait()
    for half in range(2):
        received = sq_recv.at[half]
        pltpu.make_async_copy(received, received, s_send.at[half]).wait()
    for stage in range(STAGES):
        sent = sendbuf.at[stage, pl.ds(0, n_seq - 1)]
        pltpu.make_async_copy(sent, sent, a_send.at[stage]).wait()
        own_pages(stage).wait()
        pages = pagebuf.at[stage, pl.ds(0, (n_seq - 1) * SLOTS)]
        pltpu.make_async_copy(pages, pages, p_send.at[stage]).wait()
        pltpu.make_async_copy(pages, pages, p_recv.at[stage]).wait()


def shards(n_seq, n_head, queries, key_rows, value_rows, decay_log, norm_gain, page_owner):
    toks, width = queries.shape
    heads = decay_log.shape[0]
    chunks = toks // CHUNK
    classes = heads // STAGES
    rows = HD * classes // n_seq
    n_pages = page_owner.shape[0]
    order = jnp.arange(n_pages, dtype=jnp.int32)
    earlier = (page_owner[:, None] == page_owner[None, :]) & (order[:, None] < order[None, :])
    slot = jnp.sum(earlier.astype(jnp.int32), axis=0)
    target = page_owner * SLOTS + slot
    wanted = target[None, :] == jnp.arange(n_seq * SLOTS, dtype=jnp.int32)[:, None]
    index = jnp.sum(jnp.where(wanted, order[None, :] + 1, 0), axis=1).astype(jnp.int32)
    anywhere = pl.BlockSpec(memory_space=pl.ANY)
    dma = pltpu.SemaphoreType.DMA
    return pl.pallas_call(
        functools.partial(kernel, n_seq, n_head),
        out_shape=(
            jax.ShapeDtypeStruct((toks, width), BF),
            jax.ShapeDtypeStruct((SLOTS, heads, HD, HD), BF),
        ),
        in_specs=[pl.BlockSpec(memory_space=pltpu.SMEM)]
        + [pl.BlockSpec(memory_space=pltpu.HBM)] * 5,
        out_specs=(anywhere, anywhere),
        scratch_shapes=[
            pltpu.VMEM((heads, toks, HD), BF),
            pltpu.VMEM((heads, toks, HD), BF),
            pltpu.VMEM((heads, toks, HD), BF),
            pltpu.VMEM((heads, toks, HD), F32),
            pltpu.VMEM((heads, toks, HD), F32),
            pltpu.VMEM((toks, width), BF),
            pltpu.VMEM((heads * chunks, HD, HD), BF),
            pltpu.VMEM((heads, toks), F32),
            pltpu.VMEM((heads, HD), F32),
            pltpu.VMEM((heads, 1, toks), F32),
            pltpu.VMEM((heads, 1, toks), F32),
            pltpu.VMEM((heads * chunks, 1, 128), F32),
            pltpu.VMEM((heads * chunks, 1, 128), F32),
            pltpu.VMEM((heads * chunks, 1, 128), F32),
            pltpu.VMEM((classes, STAGES, 2, 1, 128), F32),
            pltpu.VMEM((n_seq, STAGES, 2, 1, 128), F32),
            pltpu.VMEM((STAGES, n_seq, 2, rows, HD), BF),
            pltpu.VMEM((STAGES, n_seq, 2, rows, HD), BF),
            pltpu.VMEM((n_pages + 1, STAGES, rows, HD), BF),
            pltpu.VMEM((STAGES, n_seq * SLOTS, rows, HD), BF),
            pltpu.VMEM((STAGES, classes, HD, HD), BF),
            pltpu.VMEM((2, 8, 1, 128), F32),
            pltpu.VMEM((2, n_head - 1, 8, 1, 128), F32),
            pltpu.VMEM((8, 1, 128), F32),
            dma((2, heads)),
            dma((heads,)),
            dma((2,)),
            dma,
            dma,
            dma((STAGES,)),
            dma((STAGES,)),
            dma,
            dma,
            dma((STAGES,)),
            dma((STAGES,)),
            dma((STAGES,)),
            dma((2,)),
            dma((2,)),
            dma,
        ],
        compiler_params=pltpu.CompilerParams(
            collective_id=0, has_side_effects=True, vmem_limit_bytes=48 * 1024 * 1024
        ),
    )(
        index,
        queries,
        key_rows,
        value_rows,
        pltpu.with_memory_space_constraint(decay_log, pltpu.HBM),
        pltpu.with_memory_space_constraint(norm_gain.reshape(heads, HD), pltpu.HBM),
    )


def solution(mesh):
    return jax.shard_map(
        functools.partial(shards, mesh.shape["seq"], mesh.shape["head"]),
        mesh=mesh,
        in_specs=(
            P("seq", "head"),
            P("seq", "head"),
            P("seq", "head"),
            P("head", "seq"),
            P("head"),
            P(),
        ),
        out_specs=(P("seq", "head"), P("seq", "head", None, None)),
        check_vma=False,
    )
```

time: 53.4 us -> 46.2 us (0.87)
  the two profiles are of different devices: /device:TPU:6 before, /device:TPU:2 now
where the time goes in v2:
time: 46.2 us; the launch traced here: 46.1 us
  Pallas kernels  40.8 us (88%)
  local copies, waits for them, and re-layouts  3.07 us (7%)
  other arithmetic  1.58 us (3%)
  between operations  0.64 us (1%)
    pallas_call x1, Pallas kernels, shards(): pl.pallas_call(functools.partial(kernel, n_seq, n_head), out_shape=(jax.S...  40.8 us
    unnamed x2, local copies, waits for them, and re-layouts  3.07 us

profile of v2, /device:TPU:2, one launch (start us, length us, event | category | flops | bytes accessed | tf_op | source)
XLA Modules:
  0.0 46.1 jit_solution(1898705832354660365)
XLA Ops:
  0.6 0.8 %convert_reduce_fusion = s32[64]{0:T(128)S(1)} fusion(s32[64]{0:T(128)} %param.11), kind=kLoop, calls=%fused_computation.2 | loop fusion | flops 20416 | bytes 512 | tf_op jit(solution)/shard_map/reduce_sum | solution.py:470
  1.5 0.7 %iota_add_fusion = (s32[64]{0:T(128)S(1)}, s32[64]{0:T(128)S(1)}) fusion(s32[64]{0:T(128)S(1)} %convert_reduce_fusion, s32[64]{0:T(128)} %param.11), kind=kLoop, calls=%fused_computation.5 | loop fusion | flops 192 | bytes 1024 | tf_op jit(solution)/shard_map/add | solution.py:473
  2.1 0.1 select_reduce_fusion.idx_ref
  2.2 40.8 %shard_map.77 = (bf16[2048,1024]{1,0:T(8,128)(2,1)S(1)}, bf16[5,8,128,128]{3,2,1,0:T(8,128)(2,1)S(1)}) custom-call(s32[160]{0:T(256)S(1)} %select_reduce_fusion.idx_ref, bf16[2048,1024]{1,0:T(8,128)(2,1)} %q_hbm.1, bf16[2048,1024]{1,0:T(8,128)(2,1)} %k_hbm.1, bf16[2048,1024]{1,0:T(8,128)(2,1)} %v_hbm.1, f32[8,2048]{1,0:T(8,128)} %d_hbm.1, f32[8,128]{1,0:T(8,128)} %bitcast.1), custom_call_target="tpu_custom_call" | custom-call | tf_op jit(solution)/shard_map/pallas_call | solution.py:476
  43.0 2.0 %copy.10 = bf16[2048,1024]{1,0:T(8,128)(2,1)} copy(bf16[2048,1024]{1,0:T(8,128)(2,1)S(1)} %get-tuple-element.6) | data formatting | bytes 8388608
  45.0 1.1 %copy.11 = bf16[5,8,128,128]{3,2,1,0:T(8,128)(2,1)} copy(bf16[5,8,128,128]{3,2,1,0:T(8,128)(2,1)S(1)} %get-tuple-element.7) | data formatting | bytes 2621440

commit v3 on v2

--- a/solution.py
+++ b/solution.py
@@ -37,12 +37,12 @@
 def kernel(
     n_seq,
     n_head,
-    idx_ref,
     q_hbm,
     k_hbm,
     v_hbm,
     d_hbm,
     g_hbm,
+    owner_hbm,
     att_hbm,
     cache_hbm,
     qb,
@@ -54,6 +54,9 @@
     sl,
     d_ref,
     g_ref,
+    owner_ref,
+    idx_vec,
+    idx_ref,
     c_ref,
     f_ref,
     a_ref,
@@ -137,13 +140,19 @@
 
     d_copy = pltpu.make_async_copy(d_hbm, d_ref, small_sem.at[0])
     g_copy = pltpu.make_async_copy(g_hbm, g_ref, small_sem.at[1])
+    owner_copy = pltpu.make_async_copy(owner_hbm, owner_ref, small_sem.at[2])
+    idx_copy = pltpu.make_async_copy(idx_vec, idx_ref, small_sem.at[3])
     d_copy.start()
-    for stage in range(STAGES):
-
+    owner_copy.start()
+
+    def load(stage):
         @pl.loop(0, classes)
         def _(s):
             for copy in kv_copies(stage, s):
                 copy.start()
+
+    load(0)
+    load(1)
 
     barrier = pltpu.get_barrier_semaphore()
 
@@ -338,7 +347,7 @@
     def hand_out(stage):
         def fill(i):
             for s in range(SLOTS):
-                pagebuf[stage, i * SLOTS + s] = snap[idx_ref[i * SLOTS + s], stage]
+                pagebuf[stage, i * SLOTS + s] = snap[idx_ref[0, i * SLOTS + s], stage]
 
         def visit(i):
             fill(i)
@@ -347,6 +356,27 @@
         each_other(visit)
         fill(me)
         own_pages(stage).start()
+
+    owner_copy.wait()
+    n_pages = owner_ref.shape[1]
+    square = (n_pages, n_pages)
+    above = lax.broadcasted_iota(jnp.int32, square, 0)
+    across = lax.broadcasted_iota(jnp.int32, square, 1)
+
+    def turned(row):
+        spread = jnp.broadcast_to(row, square)
+        return jnp.max(jnp.where(above == across, spread, 0), axis=1, keepdims=True)
+
+    owner = owner_ref[...]
+    same = (turned(owner) == owner) & (above < across)
+    slot = jnp.sum(jnp.where(same, 1, 0), axis=0, keepdims=True)
+    target = turned(owner * SLOTS + slot)
+    wide = (n_pages, 256)
+    page = lax.broadcasted_iota(jnp.int32, wide, 0)
+    place = lax.broadcasted_iota(jnp.int32, wide, 1)
+    found = jnp.where(target == place, page + 1, 0)
+    idx_vec[...] = jnp.max(found, axis=0, keepdims=True)
+    idx_copy.start()
 
     states(0)
     pl.semaphore_wait(barrier, n_seq - 1 + n_head - 1)
@@ -363,6 +393,7 @@
     pl.loop(0, FIRST)(intra)
     all_decays = dec_recv.at[pl.ds(0, n_seq - 1)]
     pltpu.make_async_copy(all_decays, all_decays, d_recv).wait()
+    idx_copy.wait()
     wait_rows(0)
     recur(0)
     hand_out(0)
@@ -465,12 +496,6 @@
     classes = heads // STAGES
     rows = HD * classes // n_seq
     n_pages = page_owner.shape[0]
-    order = jnp.arange(n_pages, dtype=jnp.int32)
-    earlier = (page_owner[:, None] == page_owner[None, :]) & (order[:, None] < order[None, :])
-    slot = jnp.sum(earlier.astype(jnp.int32), axis=0)
-    target = page_owner * SLOTS + slot
-    wanted = target[None, :] == jnp.arange(n_seq * SLOTS, dtype=jnp.int32)[:, None]
-    index = jnp.sum(jnp.where(wanted, order[None, :] + 1, 0), axis=1).astype(jnp.int32)
     anywhere = pl.BlockSpec(memory_space=pl.ANY)
     dma = pltpu.SemaphoreType.DMA
     return pl.pallas_call(
@@ -479,8 +504,7 @@
             jax.ShapeDtypeStruct((toks, width), BF),
             jax.ShapeDtypeStruct((SLOTS, heads, HD, HD), BF),
         ),
-        in_specs=[pl.BlockSpec(memory_space=pltpu.SMEM)]
-        + [pl.BlockSpec(memory_space=pltpu.HBM)] * 5,
+        in_specs=[pl.BlockSpec(memory_space=pltpu.HBM)] * 6,
         out_specs=(anywhere, anywhere),
         scratch_shapes=[
             pltpu.VMEM((heads, toks, HD), BF),
@@ -492,6 +516,9 @@
             pltpu.VMEM((heads * chunks, HD, HD), BF),
             pltpu.VMEM((heads, toks), F32),
             pltpu.VMEM((heads, HD), F32),
+            pltpu.VMEM((1, n_pages), jnp.int32),
+            pltpu.VMEM((1, 256), jnp.int32),
+            pltpu.SMEM((1, 256), jnp.int32),
             pltpu.VMEM((heads, 1, toks), F32),
             pltpu.VMEM((heads, 1, toks), F32),
             pltpu.VMEM((heads * chunks, 1, 128), F32),
@@ -509,7 +536,7 @@
             pltpu.VMEM((8, 1, 128), F32),
             dma((2, heads)),
             dma((heads,)),
-            dma((2,)),
+            dma((4,)),
             dma,
             dma,
             dma((STAGES,)),
@@ -527,12 +554,12 @@
             collective_id=0, has_side_effects=True, vmem_limit_bytes=48 * 1024 * 1024
         ),
     )(
-        index,
         queries,
         key_rows,
         value_rows,
         pltpu.with_memory_space_constraint(decay_log, pltpu.HBM),
         pltpu.with_memory_space_constraint(norm_gain.reshape(heads, HD), pltpu.HBM),
+        pltpu.with_memory_space_constraint(page_owner.reshape(1, n_pages), pltpu.HBM),
     )
 
 

time: 46.2 us -> 42 us (0.909)
  the two profiles are of different devices: /device:TPU:2 before, /device:TPU:1 now
where the time goes in v3:
time: 42 us; the launch traced here: 41.2 us
  Pallas kernels  37.5 us (89%)
  local copies, waits for them, and re-layouts  3.07 us (7%)
  between operations  0.64 us (2%)
    pallas_call x1, Pallas kernels, shards(): pl.pallas_call(functools.partial(kernel, n_seq, n_head), out_shape=(jax.S...  37.5 us
    unnamed x2, local copies, waits for them, and re-layouts  3.07 us

profile of v3, /device:TPU:1, one launch (start us, length us, event | category | flops | bytes accessed | tf_op | source)
XLA Modules:
  0.0 41.2 jit_solution(17226349673436611402)
XLA Ops:
  0.6 37.5 %shard_map.77 = (bf16[2048,1024]{1,0:T(8,128)(2,1)S(1)}, bf16[5,8,128,128]{3,2,1,0:T(8,128)(2,1)S(1)}) custom-call(bf16[2048,1024]{1,0:T(8,128)(2,1)} %q_hbm.1, bf16[2048,1024]{1,0:T(8,128)(2,1)} %k_hbm.1, bf16[2048,1024]{1,0:T(8,128)(2,1)} %v_hbm.1, f32[8,2048]{1,0:T(8,128)} %d_hbm.1, f32[8,128]{1,0:T(8,128)} %bitcast.2, s32[1,64]{1,0:T(1,128)} %bitcast.3), custom_call_target="tpu_custom_call" | custom-call | tf_op jit(solution)/shard_map/pallas_call | solution.py:501
  38.1 2.0 %copy.10 = bf16[2048,1024]{1,0:T(8,128)(2,1)} copy(bf16[2048,1024]{1,0:T(8,128)(2,1)S(1)} %get-tuple-element.4) | data formatting | bytes 8388608
  40.1 1.1 %copy.11 = bf16[5,8,128,128]{3,2,1,0:T(8,128)(2,1)} copy(bf16[5,8,128,128]{3,2,1,0:T(8,128)(2,1)S(1)} %get-tuple-element.5) | data formatting | bytes 2621440

commit v4 on v3

--- a/solution.py
+++ b/solution.py
@@ -396,13 +396,13 @@
     idx_copy.wait()
     wait_rows(0)
     recur(0)
-    hand_out(0)
     pl.loop(FIRST, SECOND)(intra)
     wait_rows(1)
     recur(1)
     each_other(lambda i: send_entry(i).start())
     ent[:, mine, pl.ds(r0, rows), :] = snap[2 * me]
 
+    hand_out(0)
     hand_out(1)
     pl.loop(SECOND, heads)(intra)
 

time: 42 us -> 41.3 us (0.983); the launches traced: 41.2 us -> 41.2 us
  no operation moved by 1% of the time
where the time goes in v4:
time: 41.3 us; the launch traced here: 41.2 us
  Pallas kernels  37.5 us (91%)
  local copies, waits for them, and re-layouts  3.07 us (7%)
  between operations  0.64 us (2%)
    pallas_call x1, Pallas kernels, shards(): pl.pallas_call(functools.partial(kernel, n_seq, n_head), out_shape=(jax.S...  37.5 us
    unnamed x2, local copies, waits for them, and re-layouts  3.07 us

profile of v4, /device:TPU:1, one launch (start us, length us, event | category | flops | bytes accessed | tf_op | source)
XLA Modules:
  0.0 41.2 jit_solution(522635191691212790)
XLA Ops:
  0.6 37.5 %shard_map.77 = (bf16[2048,1024]{1,0:T(8,128)(2,1)S(1)}, bf16[5,8,128,128]{3,2,1,0:T(8,128)(2,1)S(1)}) custom-call(bf16[2048,1024]{1,0:T(8,128)(2,1)} %q_hbm.1, bf16[2048,1024]{1,0:T(8,128)(2,1)} %k_hbm.1, bf16[2048,1024]{1,0:T(8,128)(2,1)} %v_hbm.1, f32[8,2048]{1,0:T(8,128)} %d_hbm.1, f32[8,128]{1,0:T(8,128)} %bitcast.2, s32[1,64]{1,0:T(1,128)} %bitcast.3), custom_call_target="tpu_custom_call" | custom-call | tf_op jit(solution)/shard_map/pallas_call | solution.py:501
  38.1 2.0 %copy.10 = bf16[2048,1024]{1,0:T(8,128)(2,1)} copy(bf16[2048,1024]{1,0:T(8,128)(2,1)S(1)} %get-tuple-element.4) | data formatting | bytes 8388608
  40.1 1.1 %copy.11 = bf16[5,8,128,128]{3,2,1,0:T(8,128)(2,1)} copy(bf16[5,8,128,128]{3,2,1,0:T(8,128)(2,1)S(1)} %get-tuple-element.5) | data formatting | bytes 2621440
